TPU v7x, 512 devices: a whole 4x8x8 slice. The times are simulated.
512 devices in a mesh: region: 32 (over x, y), shard: 16 (over z, core).
Axes of the slice: x: 4, y: 8, z: 8, core: 2. Of those that a mesh axis runs over, the one named last changes fastest.
Arguments:
- planes: bfloat16 [4, 16384, 512], P(None, ('region', 'shard')), may hold values from -6 to 6
- sed_weights: float32 [6, 4], replicated, may hold values from 0.1 to 2
- psf_taps: float32 [2, 6, 3, 25], replicated, may hold values from 0.004 to 0.08
- resample_rows: bfloat16 [16384, 128, 128], P(('region', 'shard')), may hold values from -0.5 to 0.5
- resample_cols: bfloat16 [16384, 128, 256], P(('region', 'shard')), may hold values from -0.375 to 0.375
- observed: bfloat16 [16384, 128, 128], P(('region', 'shard')), may hold values from -6 to 6
- exposure_meta: int32 [3, 16384], P(None, 'region'), may hold values from 0 to 15, as said below
- slot_counts: int32 [32, 16], P('region'), may hold values from 8 to 32, as said below
Outputs:
- plane_grad: float32 [4, 16384, 512], P(None, ('region', 'shard'))
Inputs may be any that keep to these rules, and one draw needn't show every extreme that they name: `exposure_meta`: row 0 is a row tile of the exposure's region, 0 to 15; row 1 a column tile, 0 to 1; row 2 a band, 0 to 5. `slot_counts`: the live slots of a device are its first ones. In every region one device has all 32 slots live, the others between 8 and 16.
All inputs are finite; a program needn't handle non-finite values.
Results may differ from a plain program's by a relative error of at most 0.003.
Values may be sent and summed in bfloat16 or wider, within the bound.
A program may use at most 64 MiB of HBM per device.

v0:
```python
import jax
import jax.numpy as jnp
from jax import lax
from jax.sharding import PartitionSpec as P

GROUP = 4


def passed_along(block, axis, distance):
    devices = range(lax.axis_size(axis))
    route = [(i - distance, i) for i in devices if i - distance in devices]
    return lax.ppermute(block, axis, route)


def band_tables(taps, width):
    tap_count = taps.shape[-1]
    offset = (
        jnp.arange(width, dtype=jnp.int32)[:, None]
        - jnp.arange(width, dtype=jnp.int32)[None, :]
        + tap_count // 2
    )
    selector = (offset[None, :, :] == jnp.arange(tap_count, dtype=jnp.int32)[:, None, None]).astype(
        jnp.float32
    )
    return jnp.einsum("btk,kij->btij", taps, selector, precision=lax.Precision.HIGHEST).astype(
        jnp.bfloat16
    )


def local(
    planes,
    sed_weights,
    psf_taps,
    resample_rows,
    resample_cols,
    observed,
    exposure_meta,
    slot_counts,
):
    shard_count = lax.axis_size("shard")
    my_index = lax.axis_index("shard")
    channel_count, tile_rows, col_total = planes.shape
    slot_count, out_rows, win_rows = resample_rows.shape
    win_cols = resample_cols.shape[2]
    region_rows = tile_rows * shard_count
    rim_rows = win_rows - tile_rows
    gathered = lax.all_gather(planes, "shard", axis=1, tiled=True)
    next_part = passed_along(gathered[:, :rim_rows], "region", -1)
    extended = jnp.concatenate([gathered, next_part], axis=1)
    rows_tab = band_tables(psf_taps[0], win_rows)
    cols_tab = band_tables(psf_taps[1], win_cols)
    live_counts = slot_counts[0]
    device_ids = jnp.arange(shard_count, dtype=jnp.int32)
    position = jnp.arange(slot_count, dtype=jnp.int32)
    my_count = jnp.sum(jnp.where(device_ids == my_index, live_counts, 0))
    row_maps, col_maps, pixel_sets = (resample_rows, resample_cols, observed)
    is_live = position < my_count
    region_slot = my_index * slot_count + position
    meta_total = exposure_meta.shape[1]
    matches = (jnp.arange(meta_total, dtype=jnp.int32)[:, None] == region_slot[None, :]).astype(
        jnp.int32
    )
    meta_sel = jnp.dot(exposure_meta, matches)
    live_rank = jnp.cumsum(is_live.astype(jnp.int32)) - 1
    picks = jnp.logical_and(is_live[:, None], live_rank[:, None] == position[None, :])
    live_order = jnp.sum(jnp.where(picks, position[:, None], 0), axis=0)
    live_total = jnp.sum(is_live.astype(jnp.int32))
    turn_total = (live_total + GROUP - 1) // GROUP

    def cut_window(start_row, start_col):
        return lax.dynamic_slice(
            extended, (jnp.int32(0), start_row, start_col), (channel_count, win_rows, win_cols)
        )

    def visit(turn_index, gradient):
        ranks = turn_index * GROUP + jnp.arange(GROUP, dtype=jnp.int32)
        usable = ranks < live_total
        chosen = jnp.take(live_order, jnp.minimum(ranks, slot_count - 1))
        row_start = jnp.take(meta_sel[0], chosen) * tile_rows
        col_start = jnp.take(meta_sel[1], chosen) * win_cols
        band_of = jnp.take(meta_sel[2], chosen)
        windows = jax.vmap(cut_window)(row_start, col_start)
        sed_sel = jnp.take(sed_weights, band_of, axis=0)
        py_mat = jnp.take(rows_tab, band_of, axis=0)
        px_mat = jnp.take(cols_tab, band_of, axis=0)
        ry_mat = jnp.take(row_maps, chosen, axis=0)
        rx_mat = jnp.take(col_maps, chosen, axis=0)
        pixels = jnp.take(pixel_sets, chosen, axis=0)
        mixed = jnp.sum(sed_sel[:, :, None, None] * windows.astype(jnp.float32), axis=1).astype(
            jnp.bfloat16
        )
        smeared = jnp.einsum(
            "gtiy,gyx->gtix", py_mat, mixed, preferred_element_type=jnp.float32
        ).astype(jnp.bfloat16)
        blurred = jnp.einsum(
            "gtix,gtjx->gij", smeared, px_mat, preferred_element_type=jnp.float32
        ).astype(jnp.bfloat16)
        sampled = jnp.einsum(
            "goy,gyx->gox", ry_mat, blurred, preferred_element_type=jnp.float32
        ).astype(jnp.bfloat16)
        model = jnp.einsum("gox,gpx->gop", sampled, rx_mat, preferred_element_type=jnp.float32)
        misfit = (model - pixels.astype(jnp.float32)).astype(jnp.bfloat16)
        back_rows = jnp.einsum(
            "goy,gop->gyp", ry_mat, misfit, preferred_element_type=jnp.float32
        ).astype(jnp.bfloat16)
        back = jnp.einsum(
            "gyp,gpx->gyx", back_rows, rx_mat, preferred_element_type=jnp.float32
        ).astype(jnp.bfloat16)
        unsmeared = jnp.einsum(
            "gtiy,gix->gtyx", py_mat, back, preferred_element_type=jnp.float32
        ).astype(jnp.bfloat16)
        window_grad = jnp.einsum(
            "gtyj,gtjx->gyx", unsmeared, px_mat, preferred_element_type=jnp.float32
        )
        contrib = sed_sel[:, :, None, None] * window_grad[:, None]
        for member in range(GROUP):
            corner = (jnp.int32(0), row_start[member], col_start[member])
            current = lax.dynamic_slice(gradient, corner, (channel_count, win_rows, win_cols))
            added = jnp.where(usable[member], contrib[member], 0.0)
            gradient = lax.dynamic_update_slice(gradient, current + added, corner)
        return gradient

    start = jnp.zeros((channel_count, region_rows + rim_rows, col_total), jnp.float32)
    gradient = lax.fori_loop(0, turn_total, visit, start)
    incoming = passed_along(gradient[:, region_rows:], "region", 1)
    own_rows = gradient[:, :region_rows].at[:, :rim_rows].add(incoming)
    return lax.psum_scatter(own_rows, "shard", scatter_dimension=1, tiled=True)


def solution(mesh):
    placed = (
        P(None, ("region", "shard"), None),
        P(),
        P(),
        P(("region", "shard"), None, None),
        P(("region", "shard"), None, None),
        P(("region", "shard"), None, None),
        P(None, "region"),
        P("region", None),
    )
    return jax.shard_map(
        local,
        mesh=mesh,
        in_specs=placed,
        out_specs=P(None, ("region", "shard"), None),
        check_vma=False,
    )
```

profile of v0, /device:TPU:2, one launch (start us, length us, event | category | flops | bytes accessed | tf_op | source)
XLA Modules:
  0.0 797.1 jit_solution(13557028132865648355)
XLA Ops:
  16.7 40.7 %all-gather.2.cloned.1.call-done = bf16[4,512,512]{2,1,0:T(8,128)(2,1)} async-done(((bf16[4,32,512]{2,1,0:T(8,128)(2,1)}), bf16[4,512,512]{2,1,0:T(8,128)(2,1)}) %all-gather.2.cloned.1.call-update) | async-done | bytes 2097168 | tf_op jit(solution)/shard_map/all_gather | solution.py:47
  59.2 4.7 collective-permute-start
  79.2 311.7 %while.14 = (s32[]{:T(128)}, f32[4,608,512]{2,1,0:T(8,128)}, s32[]{:T(128)}, s32[3,32]{1,0:T(4,128)S(1)}, s32[32]{0:T(128)S(1)}, /*index=5*/s32[]{:T(128)}, f32[...) while((s32[]{:T(128)}, f32[4,608,512]{2,1,0:T(8,128)}, ...), condition=%wide.region_6.9_spmd, body=%wide.region_4.8_spmd.sunk | while | flops 728304896 | bytes 28457620 | solution.py:124
  106.9 12.7 %while.15 = (s32[]{:T(128)}, bf16[4,608,512]{2,1,0:T(8,128)(2,1)}, s32[4,3]{1,0:T(4,128)S(1)}, bf16[4,4,128,256]{3,2,1,0:T(8,128)(2,1)S(1)}, s32[]{:T(128)}) while((s32[]{:T(128)}, bf16[4,608,512]{2,1,0:T(8,128)(2,1)}, s32[4,3]{1,0:T(4,128)S(1)}, bf16[4,4,128,256]{3,2,1,0:T(8,128)(2,1)S(1)}, s32[]{:T(128)}) %tuple.81), condition=%wide.while_cond.1, body=%wide.while_body.1.sunk | while | flops 2 | bytes 524413 | solution.py:71
  129.5 5.3 dynamic_update_slice.16
  136.7 5.3 dynamic_update_slice.17
  143.8 5.2 dynamic_update_slice.18
  151.0 5.2 dynamic_update_slice.19
  184.0 12.9 %while.15 = (s32[]{:T(128)}, bf16[4,608,512]{2,1,0:T(8,128)(2,1)}, s32[4,3]{1,0:T(4,128)S(1)}, bf16[4,4,128,256]{3,2,1,0:T(8,128)(2,1)S(1)}, s32[]{:T(128)}) while((s32[]{:T(128)}, bf16[4,608,512]{2,1,0:T(8,128)(2,1)}, s32[4,3]{1,0:T(4,128)S(1)}, bf16[4,4,128,256]{3,2,1,0:T(8,128)(2,1)S(1)}, s32[]{:T(128)}) %tuple.81), condition=%wide.while_cond.1, body=%wide.while_body.1.sunk | while | flops 2 | bytes 524413 | solution.py:71
  206.8 5.9 dynamic_update_slice.16
  214.6 5.3 dynamic_update_slice.17
  221.8 5.9 dynamic_update_slice.18
  229.8 5.9 dynamic_update_slice.19
  263.4 12.9 %while.15 = (s32[]{:T(128)}, bf16[4,608,512]{2,1,0:T(8,128)(2,1)}, s32[4,3]{1,0:T(4,128)S(1)}, bf16[4,4,128,256]{3,2,1,0:T(8,128)(2,1)S(1)}, s32[]{:T(128)}) while((s32[]{:T(128)}, bf16[4,608,512]{2,1,0:T(8,128)(2,1)}, s32[4,3]{1,0:T(4,128)S(1)}, bf16[4,4,128,256]{3,2,1,0:T(8,128)(2,1)S(1)}, s32[]{:T(128)}) %tuple.81), condition=%wide.while_cond.1, body=%wide.while_body.1.sunk | while | flops 2 | bytes 524413 | solution.py:71
  286.3 5.9 dynamic_update_slice.16
  294.1 5.9 dynamic_update_slice.17
  307.9 5.8 dynamic_update_slice.19
  341.4 12.7 %while.15 = (s32[]{:T(128)}, bf16[4,608,512]{2,1,0:T(8,128)(2,1)}, s32[4,3]{1,0:T(4,128)S(1)}, bf16[4,4,128,256]{3,2,1,0:T(8,128)(2,1)S(1)}, s32[]{:T(128)}) while((s32[]{:T(128)}, bf16[4,608,512]{2,1,0:T(8,128)(2,1)}, s32[4,3]{1,0:T(4,128)S(1)}, bf16[4,4,128,256]{3,2,1,0:T(8,128)(2,1)S(1)}, s32[]{:T(128)}) %tuple.81), condition=%wide.while_cond.1, body=%wide.while_body.1.sunk | while | flops 2 | bytes 524413 | solution.py:71
  364.1 5.3 dynamic_update_slice.16
  371.2 5.3 dynamic_update_slice.17
  378.3 5.3 dynamic_update_slice.18
  385.6 5.3 dynamic_update_slice.19
  398.6 9.4 %collective-permute-done.1 = f32[4,96,512]{2,1,0:T(8,128)S(1)} collective-permute-done((f32[4,96,512]{2,1,0:T(8,128)S(1)}, f32[4,96,512]{2,1,0:T(8,128)S(1)}, u32[]{:S(2)}, u32[]{:S(2)}) %collective-permute-start.1) | collective-permute-done | bytes 786464 | tf_op jit(solution)/shard_map/ppermute | solution.py:12
  410.3 380.0 %reduce-scatter.2.cloned.1.call-done = f32[4,32,512]{2,1,0:T(8,128)} async-done(((f32[4,512,512]{2,1,0:T(8,128)}), f32[4,32,512]{2,1,0:T(8,128)}) %reduce-scatter.2.cloned.1.call-update) | async-done | bytes 262160 | tf_op jit(solution)/shard_map/reduce_scatter | solution.py:127
  (236 shorter events, 203.8 us)
Async XLA Ops:
  6.5 63.7 %copy-start = (s32[3,512]{1,0:T(4,128)S(1)}, s32[3,512]{1,0:T(4,128)}, u32[]{:S(2)}) copy-start(s32[3,512]{1,0:T(4,128)} %param.22) | copy-start | bytes 18436
  6.5 50.8 %all-gather.2.cloned.1.call-start = ((), (), s32[]{:S(2)}) async-start(), calls=%async_computation.1 | async-start | bytes 2228224 | tf_op jit(solution)/shard_map/all_gather | solution.py:47
  7.3 783.0 %reduce-scatter.2.cloned.1.call-start = ((), (), s32[]{:S(2)}) async-start(), calls=%async_computation.2 | async-start | bytes 4456448 | tf_op jit(solution)/shard_map/reduce_scatter | solution.py:127
  12.8 53.1 %copy-start.3 = (f32[6,4]{0,1:T(4,128)S(1)}, f32[6,4]{0,1:T(4,128)}, u32[]{:S(2)}) copy-start(f32[6,4]{0,1:T(4,128)} %param.17) | copy-start | bytes 292
  59.2 13.8 %collective-permute-start = (bf16[4,96,512]{2,1,0:T(8,128)(2,1)}, bf16[4,96,512]{2,1,0:T(8,128)(2,1)}, u32[]{:S(2)}, u32[]{:S(2)}) collective-permute-start(bf16[4,96,512]{2,1,0:T(8,128)(2,1)} %slice.142), channel_id=1, source_target_pairs={{16,0},{32,16},{48,32},{64,48},{80,64},{96,80},{112,96},{128,112},... | collective-permute-start | bytes 1179656 | tf_op jit(solution)/shard_map/ppermute | solution.py:12
  76.3 2.8 copy-start.1
  106.9 15.4 %copy-start.2 = (bf16[4,3,128,128]{3,2,1,0:T(8,128)(2,1)}, bf16[4,3,128,128]{3,2,1,0:T(8,128)(2,1)S(1)}, u32[]{:S(2)}) copy-start(bf16[4,3,128,128]{3,2,1,0:T(8,128)(2,1)S(1)} %gather_fusion.6) | copy-start | bytes 1179652 | tf_op jit(solution)/shard_map/while
  183.9 15.5 %copy-start.2 = (bf16[4,3,128,128]{3,2,1,0:T(8,128)(2,1)}, bf16[4,3,128,128]{3,2,1,0:T(8,128)(2,1)S(1)}, u32[]{:S(2)}) copy-start(bf16[4,3,128,128]{3,2,1,0:T(8,128)(2,1)S(1)} %gather_fusion.6) | copy-start | bytes 1179652 | tf_op jit(solution)/shard_map/while
  263.4 15.5 %copy-start.2 = (bf16[4,3,128,128]{3,2,1,0:T(8,128)(2,1)}, bf16[4,3,128,128]{3,2,1,0:T(8,128)(2,1)S(1)}, u32[]{:S(2)}) copy-start(bf16[4,3,128,128]{3,2,1,0:T(8,128)(2,1)S(1)} %gather_fusion.6) | copy-start | bytes 1179652 | tf_op jit(solution)/shard_map/while
  341.4 15.4 %copy-start.2 = (bf16[4,3,128,128]{3,2,1,0:T(8,128)(2,1)}, bf16[4,3,128,128]{3,2,1,0:T(8,128)(2,1)S(1)}, u32[]{:S(2)}) copy-start(bf16[4,3,128,128]{3,2,1,0:T(8,128)(2,1)S(1)} %gather_fusion.6) | copy-start | bytes 1179652 | tf_op jit(solution)/shard_map/while
  392.0 16.0 %collective-permute-start.1 = (f32[4,96,512]{2,1,0:T(8,128)S(1)}, f32[4,96,512]{2,1,0:T(8,128)S(1)}, u32[]{:S(2)}, u32[]{:S(2)}) collective-permute-start(f32[4,96,512]{2,1,0:T(8,128)S(1)} %slice.102), channel_id=1, source_target_pairs={{0,16},{16,32},{32,48},{48,64},{64,80},{80,96},{96,112},{112,128},... | collective-permute-start | bytes 2359304 | tf_op jit(solution)/shard_map/ppermute | solution.py:12
Sparse Core Ops, SparseCore 0:
  9.5 47.8 all-gather.1
  410.4 379.8 reduce-scatter.1
where the time goes:
time: 809 us; the launch traced here: 797 us
  waiting for transfers between devices  433 us (54%)
  local copies, waits for them, and re-layouts  208 us (26%)
  loops' own time  61.7 us (8%)
  other arithmetic  46.3 us (6%)
  matrix products  26.5 us (3%)
  between operations  14.2 us (2%)
    reduce_scatter x1, waiting for transfers between devices, local(): return lax.psum_scatter(own_rows, 'shard', scatter_dimension=1, tiled=True)  380 us
    dynamic_update_slice x16, local copies, waits for them, and re-layouts, visit(): gradient = lax.dynamic_update_slice(gradient, current + added, corner)  86.5 us
    another operation x1, loops' own time, local(): gradient = lax.fori_loop(0, turn_total, visit, start)  61.2 us
    gather x48, local copies, waits for them, and re-layouts  50.8 us
    all_gather x1, waiting for transfers between devices, local(): gathered = lax.all_gather(planes, 'shard', axis=1, tiled=True)  40.7 us
    add x16, other arithmetic, visit(): gradient = lax.dynamic_update_slice(gradient, current + added, corner)  30.8 us
  transfers between devices with their start and end apart: 4, of which 4 were waited for; matrix products, arithmetic and copies ran while one was open for 2% of the time, Pallas kernels for 0%

commit v1 on v0

--- a/solution.py
+++ b/solution.py
@@ -37,6 +37,21 @@
     exposure_meta,
     slot_counts,
 ):
+
+    def render_forms(xin):
+        extent = lax.axis_size("shard")
+        so_far_all = [xin]
+        for dev_j in range(extent - 1):
+            mixed_arr = lax.ppermute(
+                so_far_all[-1],
+                axis_name="shard",
+                perm=[(h, (h + 1) % extent) for h in range(extent)],
+            )
+            so_far_all.append(mixed_arr)
+        tall = jnp.concatenate(so_far_all[::-1], axis=1)
+        z_new = lax.axis_index("shard")
+        return jnp.roll(tall, (z_new + 1) * xin.shape[1], axis=1)
+
     shard_count = lax.axis_size("shard")
     my_index = lax.axis_index("shard")
     channel_count, tile_rows, col_total = planes.shape
@@ -44,7 +59,7 @@
     win_cols = resample_cols.shape[2]
     region_rows = tile_rows * shard_count
     rim_rows = win_rows - tile_rows
-    gathered = lax.all_gather(planes, "shard", axis=1, tiled=True)
+    gathered = render_forms(planes)
     next_part = passed_along(gathered[:, :rim_rows], "region", -1)
     extended = jnp.concatenate([gathered, next_part], axis=1)
     rows_tab = band_tables(psf_taps[0], win_rows)

time: 809 us -> 869 us (1.074)
  the two profiles are of different devices: /device:TPU:2 before, /device:TPU:10 now
where the time goes in v1:
time: 869 us; the launch traced here: 858 us
  waiting for transfers between devices  534 us (61%)
  local copies, waits for them, and re-layouts  199 us (23%)
  loops' own time  43.6 us (5%)
  other arithmetic  40 us (5%)
  matrix products  21.3 us (2%)
  between operations  14.3 us (2%)
    reduce_scatter x1, waiting for transfers between devices, local(): return lax.psum_scatter(own_rows, 'shard', scatter_dimension=1, tiled=True)  370 us
    ppermute x2, waiting for transfers between devices, passed_along(): return lax.ppermute(block, axis, route)  86.2 us
    ppermute x15, waiting for transfers between devices, render_forms(): lax.ppermute(so_far_all[-1], axis_name='shard', perm=[(h, (h + 1) % exten...  77.9 us
    dynamic_update_slice x12, local copies, waits for them, and re-layouts, visit(): gradient = lax.dynamic_update_slice(gradient, current + added, corner)  63 us
    another operation x1, loops' own time, local(): gradient = lax.fori_loop(0, turn_total, visit, start)  43.2 us
    unnamed x77, local copies, waits for them, and re-layouts  41.1 us
    gather x36, local copies, waits for them, and re-layouts  35.8 us
    add x12, other arithmetic, visit(): gradient = lax.dynamic_update_slice(gradient, current + added, corner)  23.2 us
  transfers between devices with their start and end apart: 18, of which 17 were waited for; matrix products, arithmetic and copies ran while one was open for 3% of the time, Pallas kernels for 0%

profile of v1, /device:TPU:10, one launch (start us, length us, event | category | flops | bytes accessed | tf_op | source)
XLA Modules:
  0.0 857.6 jit_solution(5440675356321508059)
XLA Ops:
  6.6 11.3 %collective-permute-done = bf16[4,32,512]{2,1,0:T(8,128)(2,1)S(1)} collective-permute-done((bf16[4,32,512]{2,1,0:T(8,128)(2,1)}, bf16[4,32,512]{2,1,0:T(8,128)(2,1)S(1)}, u32[]{:S(2)}, u32[]{:S(2)}) %collective-permute-start) | collective-permute-done | bytes 131104 | tf_op jit(solution)/shard_map/ppermute | solution.py:45
  17.9 5.6 collective-permute-done.1
  23.5 5.6 collective-permute-done.2
  29.8 5.6 collective-permute-done.3
  36.0 5.6 collective-permute-done.4
  42.3 5.6 collective-permute-done.5
  48.6 5.6 collective-permute-done.6
  54.9 5.6 collective-permute-done.7
  61.1 5.6 collective-permute-done.8
  67.4 5.6 collective-permute-done.9
  157.1 226.5 %while.14 = (s32[]{:T(128)}, f32[4,608,512]{2,1,0:T(8,128)}, s32[]{:T(128)}, s32[3,32]{1,0:T(4,128)S(1)}, s32[32]{0:T(128)S(1)}, /*index=5*/s32[]{:T(128)}, f32[...) while((s32[]{:T(128)}, f32[4,608,512]{2,1,0:T(8,128)}, ...), condition=%wide.region_6.9_spmd, body=%wide.region_4.8_spmd.sunk | while | flops 728304896 | bytes 28457620 | solution.py:139
  183.8 12.0 %while.15 = (s32[]{:T(128)}, bf16[4,608,512]{2,1,0:T(8,128)(2,1)}, s32[4,3]{1,0:T(4,128)S(1)}, bf16[4,4,128,256]{3,2,1,0:T(8,128)(2,1)S(1)}, s32[]{:T(128)}) while((s32[]{:T(128)}, bf16[4,608,512]{2,1,0:T(8,128)(2,1)}, s32[4,3]{1,0:T(4,128)S(1)}, bf16[4,4,128,256]{3,2,1,0:T(8,128)(2,1)S(1)}, s32[]{:T(128)}) %tuple.81), condition=%wide.while_cond.1, body=%wide.while_body.1.sunk | while | flops 2 | bytes 524413 | solution.py:86
  205.8 5.2 dynamic_update_slice.16
  218.7 5.2 dynamic_update_slice.18
  257.7 12.1 %while.15 = (s32[]{:T(128)}, bf16[4,608,512]{2,1,0:T(8,128)(2,1)}, s32[4,3]{1,0:T(4,128)S(1)}, bf16[4,4,128,256]{3,2,1,0:T(8,128)(2,1)S(1)}, s32[]{:T(128)}) while((s32[]{:T(128)}, bf16[4,608,512]{2,1,0:T(8,128)(2,1)}, s32[4,3]{1,0:T(4,128)S(1)}, bf16[4,4,128,256]{3,2,1,0:T(8,128)(2,1)S(1)}, s32[]{:T(128)}) %tuple.81), condition=%wide.while_cond.1, body=%wide.while_body.1.sunk | while | flops 2 | bytes 524413 | solution.py:86
  279.8 5.3 dynamic_update_slice.16
  294.1 5.7 dynamic_update_slice.18
  301.7 5.2 dynamic_update_slice.19
  333.6 12.1 %while.15 = (s32[]{:T(128)}, bf16[4,608,512]{2,1,0:T(8,128)(2,1)}, s32[4,3]{1,0:T(4,128)S(1)}, bf16[4,4,128,256]{3,2,1,0:T(8,128)(2,1)S(1)}, s32[]{:T(128)}) while((s32[]{:T(128)}, bf16[4,608,512]{2,1,0:T(8,128)(2,1)}, s32[4,3]{1,0:T(4,128)S(1)}, bf16[4,4,128,256]{3,2,1,0:T(8,128)(2,1)S(1)}, s32[]{:T(128)}) %tuple.81), condition=%wide.while_cond.1, body=%wide.while_body.1.sunk | while | flops 2 | bytes 524413 | solution.py:86
  355.8 5.9 dynamic_update_slice.16
  370.8 5.7 dynamic_update_slice.18
  378.4 5.2 dynamic_update_slice.19
  392.2 86.2 %collective-permute-done.16 = f32[4,96,512]{2,1,0:T(8,128)S(1)} collective-permute-done((f32[4,96,512]{2,1,0:T(8,128)S(1)}, f32[4,96,512]{2,1,0:T(8,128)S(1)}, u32[]{:S(2)}, u32[]{:S(2)}) %collective-permute-start.16) | collective-permute-done | bytes 786464 | tf_op jit(solution)/shard_map/ppermute | solution.py:12
  480.6 370.2 %reduce-scatter.2.cloned.1.call-done = f32[4,32,512]{2,1,0:T(8,128)} async-done(((f32[4,512,512]{2,1,0:T(8,128)}), f32[4,32,512]{2,1,0:T(8,128)}) %reduce-scatter.2.cloned.1.call-update) | async-done | bytes 262160 | tf_op jit(solution)/shard_map/reduce_scatter | solution.py:142
  (281 shorter events, 238.2 us)
Async XLA Ops:
  6.5 143.1 %copy-start = (s32[3,512]{1,0:T(4,128)S(1)}, s32[3,512]{1,0:T(4,128)}, u32[]{:S(2)}) copy-start(s32[3,512]{1,0:T(4,128)} %param.22) | copy-start | bytes 18436
  6.5 79.6 %copy-start.23 = (s32[1,16]{1,0:T(1,128)S(1)}, s32[1,16]{1,0:T(1,128)}, u32[]{:S(2)}) copy-start(s32[1,16]{1,0:T(1,128)} %param.23) | copy-start | bytes 196
  6.5 844.2 %reduce-scatter.2.cloned.1.call-start = ((), (), s32[]{:S(2)}) async-start(), calls=%async_computation.1 | async-start | bytes 4456448 | tf_op jit(solution)/shard_map/reduce_scatter | solution.py:142
  6.5 11.3 %collective-permute-start = (bf16[4,32,512]{2,1,0:T(8,128)(2,1)}, bf16[4,32,512]{2,1,0:T(8,128)(2,1)S(1)}, u32[]{:S(2)}, u32[]{:S(2)}) collective-permute-start(bf16[4,32,512]{2,1,0:T(8,128)(2,1)} %param.16), channel_id=1, source_target_pairs={{0,1},{1,2},{2,3},{3,4},{4,5},{5,6},{6,7},{7,8},{8,9},{9,10},{10,1... | collective-permute-start | bytes 393224 | tf_op jit(solution)/shard_map/ppermute | solution.py:45
  17.9 5.6 collective-permute-start.1
  23.5 5.6 collective-permute-start.2
  29.8 5.6 collective-permute-start.3
  36.0 5.6 collective-permute-start.4
  42.3 5.6 collective-permute-start.5
  48.6 5.6 collective-permute-start.6
  54.9 5.6 collective-permute-start.7
  61.1 5.6 collective-permute-start.8
  67.4 5.6 collective-permute-start.9
  73.0 5.6 collective-permute-start.10
  78.6 5.7 collective-permute-start.11
  78.6 45.5 %copy-start.3 = (bf16[4,32,512]{2,1,0:T(8,128)(2,1)S(1)}, bf16[4,32,512]{2,1,0:T(8,128)(2,1)}, u32[]{:S(2)}) copy-start(bf16[4,32,512]{2,1,0:T(8,128)(2,1)} %param.16) | copy-start | bytes 393220
  84.3 5.9 collective-permute-start.12
  90.2 5.9 collective-permute-start.13
  96.2 5.9 collective-permute-start.14
  97.4 38.3 %copy-start.7 = (bf16[4,32,512]{2,1,0:T(8,128)(2,1)S(1)}, bf16[4,32,512]{2,1,0:T(8,128)(2,1)}, u32[]{:S(2)}) copy-start(bf16[4,32,512]{2,1,0:T(8,128)(2,1)} %copy-done.6) | copy-start | bytes 393220
  97.4 39.0 %copy-start.5 = (bf16[4,32,512]{2,1,0:T(8,128)(2,1)S(1)}, bf16[4,32,512]{2,1,0:T(8,128)(2,1)}, u32[]{:S(2)}) copy-start(bf16[4,32,512]{2,1,0:T(8,128)(2,1)} %copy-done.4) | copy-start | bytes 393220
  106.8 38.6 %copy-start.22 = (f32[6,4]{0,1:T(4,128)S(1)}, f32[6,4]{0,1:T(4,128)}, u32[]{:S(2)}) copy-start(f32[6,4]{0,1:T(4,128)} %param.17) | copy-start | bytes 292
  141.0 10.6 %collective-permute-start.15 = (bf16[4,96,512]{2,1,0:T(8,128)(2,1)}, bf16[4,96,512]{2,1,0:T(8,128)(2,1)}, u32[]{:S(2)}, u32[]{:S(2)}) collective-permute-start(bf16[4,96,512]{2,1,0:T(8,128)(2,1)} %constant_dynamic-slice_fusion.2), channel_id=1, source_target_pairs={{16,0},{32,16},{48,32},{64,48},{80,64},{96,80},{112,96},{128,112},... | collective-permute-start | bytes 1179656 | tf_op jit(solution)/shard_map/ppermute | solution.py:12
  384.8 93.5 %collective-permute-start.16 = (f32[4,96,512]{2,1,0:T(8,128)S(1)}, f32[4,96,512]{2,1,0:T(8,128)S(1)}, u32[]{:S(2)}, u32[]{:S(2)}) collective-permute-start(f32[4,96,512]{2,1,0:T(8,128)S(1)} %slice.102), channel_id=1, source_target_pairs={{0,16},{16,32},{32,48},{48,64},{64,80},{80,96},{96,112},{112,128},... | collective-permute-start | bytes 2359304 | tf_op jit(solution)/shard_map/ppermute | solution.py:12
  (20 other events, 322.3 us)
Sparse Core Ops, SparseCore 0:
  480.7 370.0 reduce-scatter.1
